TPU v7x, 32 devices: a whole 2x2x4 slice. The times are simulated.
32 devices in a mesh: ctx: 8 (over y, x, core), wa: 4 (over z).
Axes of the slice: x: 2, y: 2, z: 4, core: 2. Of those that a mesh axis runs over, the one named last changes fastest.
Arguments:
- block_input: bfloat16 [1024, 1088], P('ctx'), may hold values from -6 to 6
- span_table: int32 [8, 2], replicated, may hold values from 0 to 15, as said below
- doc_ids: int32 [1024], replicated, may hold values from 0 to 3, never falling along the last dimension, each value on 1 to 512 neighbouring positions
- attn_gain: float32 [1088], replicated, may hold values from 0.5 to 1.5
- attn_shift: float32 [1088], replicated, may hold values from -1.75 to 1.75
- qkv_weight: bfloat16 [1088, 3264], P('wa'), may hold values from -0.1875 to 0.1875
- query_bias: float32 [1088], replicated, may hold values from -3 to 3
- value_bias: float32 [1088], replicated, may hold values from -3 to 3
- out_weight: bfloat16 [1088, 1088], P(None, 'wa'), may hold values from -1 to 1
- out_bias: float32 [1088], replicated, may hold values from -3 to 3
- mlp_gain: float32 [1088], replicated, may hold values from 0.1 to 1.9
- mlp_shift: float32 [1088], replicated, may hold values from -1.75 to 1.75
- up_weight: bfloat16 [1088, 4352], P(None, 'wa'), may hold values from -0.1875 to 0.1875
- up_bias: float32 [4352], P('wa'), may hold values from -3 to 3
- down_weight: bfloat16 [4352, 1088], P('wa'), may hold values from -0.09375 to 0.09375
- down_bias: float32 [1088], replicated, may hold values from -6 to 6
- cotangent: bfloat16 [1024, 1088], P('ctx'), may hold values from -6 to 6
Outputs:
- block_output: bfloat16 [1024, 1088], P('ctx', 'wa')
- input_grad: bfloat16 [1024, 1088], P('ctx')
- qkv_grad: float32 [1088, 3264], P('wa', 'ctx')
- query_bias_grad: float32 [1088], replicated
- value_bias_grad: float32 [1088], replicated
- out_grad: float32 [1088, 1088], P('ctx', 'wa')
- out_bias_grad: float32 [1088], replicated
- up_grad: float32 [1088, 4352], P('ctx', 'wa')
- up_bias_grad: float32 [4352], P('wa')
- down_grad: float32 [4352, 1088], P('wa', 'ctx')
- down_bias_grad: float32 [1088], replicated
- attn_gain_grad: float32 [1088], replicated
- attn_shift_grad: float32 [1088], replicated
- mlp_gain_grad: float32 [1088], replicated
- mlp_shift_grad: float32 [1088], replicated
Inputs may be any that keep to these rules, and one draw needn't show every extreme that they name: The spans of 64 tokens are numbered in sequence order; the two spans of each row of span_table have numbers that add up to the count of spans minus one, and every span stands in exactly one row. `doc_ids`: document numbers never fall along the sequence; each document holds at most 512 tokens.
All inputs are finite; a program needn't handle non-finite values.
Results may differ from a plain program's by a relative error of at most 0.033.
Values may be sent and summed in bfloat16 or wider, within the bound.
No kernel may reach another device: no remote copies, remote signals or barrier semaphores. Data moves between devices by JAX's collectives and lax.ppermute only.
A program may use at most 320 MiB of HBM per device.

v0:
```python
import jax
import jax.numpy as jnp
from jax import lax
from jax.sharding import PartitionSpec as P

HEADS = 17
HEAD_DIM = 64
TOK_CTX = 128
SPAN = 64
norm_eps = 1e-05
root_half = 0.7071067811865476
inv_root_tau = 0.3989422804014327


def rounded(value):
    return lax.optimization_barrier(value.astype(jnp.bfloat16))


def gelu_value(pre):
    return 0.5 * pre * (1.0 + lax.erf(pre * root_half))


def gelu_slope(pre):
    return 0.5 * (1.0 + lax.erf(pre * root_half)) + pre * inv_root_tau * jnp.exp(-0.5 * pre * pre)


def norm_parts(values, gain, shift):
    center = jnp.mean(values, axis=-1, keepdims=True)
    square = jnp.mean(values * values, axis=-1, keepdims=True)
    inv_std = lax.rsqrt(square - center * center + norm_eps)
    normed = (values - center) * inv_std
    return (normed, inv_std, normed * gain + shift)


def norm_back(grad_out, normed, inv_std, gain):
    scaled = grad_out * gain
    return inv_std * (
        scaled
        - jnp.mean(scaled, axis=-1, keepdims=True)
        - normed * jnp.mean(scaled * normed, axis=-1, keepdims=True)
    )


def contract_rows(left, right):
    return lax.dot_general(
        left, right, (((0,), (0,)), ((), ())), preferred_element_type=jnp.float32
    )


def contract_cols(left, right):
    return lax.dot_general(
        left, right, (((1,), (1,)), ((), ())), preferred_element_type=jnp.float32
    )


def token_places(row_ids, span_table, doc_ids):
    owner = row_ids // TOK_CTX
    halves = row_ids % TOK_CTX // SPAN
    places = span_table[owner, halves] * SPAN + row_ids % SPAN
    return (places, doc_ids[places])


def body(
    block_input,
    span_table,
    doc_ids,
    attn_gain,
    attn_shift,
    qkv_weight,
    query_bias,
    value_bias,
    out_weight,
    out_bias,
    mlp_gain,
    mlp_shift,
    up_weight,
    up_bias,
    down_weight,
    down_bias,
    cotangent,
):
    tok_rows, model_width = block_input.shape
    wa_count = lax.axis_size("wa")
    wa_index = lax.axis_index("wa")
    ctx_index = lax.axis_index("ctx")
    col_width = model_width // wa_count
    col_start = wa_index * col_width
    score_scale = float(HEAD_DIM) ** (-0.5)
    input_f = block_input.astype(jnp.float32)
    attn_hat, attn_inv, attn_norm = norm_parts(input_f, attn_gain, attn_shift)
    normed_in = attn_norm.astype(jnp.bfloat16)
    normed_cols = lax.dynamic_slice_in_dim(normed_in, col_start, col_width, 1)
    bias_row = jnp.concatenate([query_bias, jnp.zeros_like(query_bias), value_bias])
    head_count = HEADS
    rows_here = tok_rows // wa_count
    first_row = (ctx_index * wa_count + wa_index) * rows_here
    query_index = first_row + jnp.arange(rows_here, dtype=jnp.int32)

    def row_sums(term_fn):
        return lax.psum_scatter(
            term_fn(jnp.int32(0), lax.axis_size("wa") * rows_here).astype(jnp.bfloat16),
            "wa",
            scatter_dimension=0,
            tiled=True,
        ).astype(jnp.float32)

    def row_gather(piece):
        return lax.all_gather(piece, "wa", axis=0, tiled=True)

    def qkv_term(offset, piece_len):
        return jnp.dot(normed_cols, qkv_weight, preferred_element_type=jnp.float32)

    qkv_own = (row_sums(qkv_term) + bias_row).astype(jnp.bfloat16)
    queries = qkv_own[:, :model_width]
    key_rows = qkv_own[:, model_width : 2 * model_width]
    val_rows = qkv_own[:, 2 * model_width :]

    def fold_keys(fold_fn, init):
        return fold_fn(
            init,
            (
                lax.all_gather(key_rows, ("ctx", "wa"), axis=0, tiled=True),
                lax.all_gather(val_rows, ("ctx", "wa"), axis=0, tiled=True),
            ),
            jnp.int32(0),
        )

    query_place, query_doc = token_places(query_index, span_table, doc_ids)
    query_heads = queries.reshape(rows_here, head_count, HEAD_DIM)

    def key_mask(key_index):
        key_place, key_doc = token_places(key_index, span_table, doc_ids)
        return (key_doc[None, :] == query_doc[:, None]) & (
            key_place[None, :] <= query_place[:, None]
        )

    def attend_piece(softmax_state, pieces, offset):
        row_top, row_total, out_accum = softmax_state
        key_piece, val_piece = pieces
        piece_len = key_piece.shape[0]
        allowed = key_mask(jnp.arange(piece_len, dtype=jnp.int32))
        scores = (
            jnp.einsum(
                "qhd,khd->hqk",
                query_heads,
                key_piece.reshape(piece_len, head_count, HEAD_DIM),
                preferred_element_type=jnp.float32,
            )
            * score_scale
        )
        scores = jnp.where(allowed[None], scores, -jnp.inf)
        new_top = jnp.maximum(row_top, jnp.max(scores, axis=-1))
        factor = jnp.exp(row_top - new_top)
        exp_scores = jnp.exp(scores - new_top[..., None])
        row_total = jnp.sum(exp_scores, axis=-1)
        piece_out = jnp.einsum(
            "hqk,khd->qhd",
            exp_scores.astype(jnp.bfloat16),
            val_piece.reshape(piece_len, head_count, HEAD_DIM),
            preferred_element_type=jnp.float32,
        )
        out_accum = out_accum * factor.T[..., None] + piece_out
        return (new_top, row_total, out_accum)

    init_state = (
        jnp.full((head_count, rows_here), -1e30, jnp.float32),
        jnp.zeros((head_count, rows_here), jnp.float32),
        jnp.zeros((rows_here, head_count, HEAD_DIM), jnp.float32),
    )
    row_top, row_total, out_accum = fold_keys(attend_piece, init_state)
    attn_out = rounded(
        (out_accum / row_total.T[..., None]).reshape(rows_here, head_count * HEAD_DIM)
    )
    log_norm = (row_top + jnp.log(row_total)).T
    attn_full = row_gather(attn_out)
    out_cols = lax.dynamic_slice_in_dim(out_bias, col_start, col_width, 0)
    input_cols = lax.dynamic_slice_in_dim(input_f, col_start, col_width, 1)
    resid_cols = (
        input_cols + jnp.dot(attn_full, out_weight, preferred_element_type=jnp.float32) + out_cols
    )
    resid_full = lax.all_gather(resid_cols.astype(jnp.bfloat16), "wa", axis=1, tiled=True).astype(
        resid_cols.dtype
    )
    mlp_hat, mlp_inv, mlp_norm = norm_parts(resid_full, mlp_gain, mlp_shift)
    normed_mid = mlp_norm.astype(jnp.bfloat16)
    hidden_pre = jnp.dot(normed_mid, up_weight, preferred_element_type=jnp.float32) + up_bias
    hidden_act = gelu_value(hidden_pre).astype(jnp.bfloat16)
    down_part = jnp.dot(hidden_act, down_weight, preferred_element_type=jnp.float32)
    down_cols = lax.psum_scatter(
        down_part.astype(jnp.bfloat16), "wa", scatter_dimension=1, tiled=True
    ).astype(jnp.float32)
    bias_cols = lax.dynamic_slice_in_dim(down_bias, col_start, col_width, 0)
    block_output = (resid_cols + down_cols + bias_cols).astype(jnp.bfloat16)
    grad_f = cotangent.astype(jnp.float32)
    down_bias_part = jnp.sum(grad_f, axis=0)
    down_grad_loc = contract_rows(hidden_act, cotangent)
    hidden_grad = contract_cols(cotangent, down_weight) * gelu_slope(hidden_pre)
    up_bias_part = jnp.sum(hidden_grad, axis=0)
    hidden_grad_b = hidden_grad.astype(jnp.bfloat16)
    up_grad_loc = contract_rows(hidden_grad_b, normed_mid)
    mid_grad = lax.psum(contract_cols(hidden_grad_b, up_weight).astype(jnp.bfloat16), "wa").astype(
        jnp.float32
    )
    mlp_gain_part = jnp.sum(mid_grad * mlp_hat, axis=0)
    mlp_shift_part = jnp.sum(mid_grad, axis=0)
    resid_grad = grad_f + norm_back(mid_grad, mlp_hat, mlp_inv, mlp_gain)
    out_bias_part = jnp.sum(resid_grad, axis=0)
    resid_grad_b = resid_grad.astype(jnp.bfloat16)
    grad_cols = lax.dynamic_slice_in_dim(resid_grad_b, col_start, col_width, 1)
    out_grad_loc = contract_rows(grad_cols, attn_full)

    def attn_term(offset, piece_len):
        return contract_cols(grad_cols, out_weight)

    attn_grad = rounded(row_sums(attn_term))
    grad_heads = attn_grad.reshape(rows_here, head_count, HEAD_DIM)
    out_heads = attn_out.reshape(rows_here, head_count, HEAD_DIM)
    delta = jnp.sum(grad_heads.astype(jnp.float32) * out_heads.astype(jnp.float32), axis=-1)
    log_hi = rounded(log_norm)
    log_lo = rounded(log_norm - log_hi.astype(jnp.float32))
    log_sent = log_hi.astype(jnp.float32) + log_lo.astype(jnp.float32)
    delta_hi = rounded(delta)
    delta_lo = rounded(delta - delta_hi.astype(jnp.float32))
    delta_sent = delta_hi.astype(jnp.float32) + delta_lo.astype(jnp.float32)

    def query_grad_piece(grad_acc, pieces, offset):
        key_piece, val_piece = pieces
        piece_len = key_piece.shape[0]
        allowed = key_mask(jnp.arange(piece_len, dtype=jnp.int32))
        key_heads = key_piece.reshape(piece_len, head_count, HEAD_DIM)
        scores = (
            jnp.einsum("qhd,khd->hqk", query_heads, key_heads, preferred_element_type=jnp.float32)
            * score_scale
        )
        exp_scores = jnp.exp(jnp.where(allowed[None], scores - log_sent.T[..., None], -jnp.inf))
        slopes = jnp.einsum(
            "qhd,khd->hqk",
            grad_heads,
            val_piece.reshape(piece_len, head_count, HEAD_DIM),
            preferred_element_type=jnp.float32,
        )
        score_grad = (exp_scores * (slopes - delta_sent.T[..., None])).astype(jnp.bfloat16)
        return jnp.einsum("hqk,khd->qhd", score_grad, key_heads, preferred_element_type=jnp.float32)

    zero_heads = jnp.zeros((rows_here, head_count, HEAD_DIM), jnp.float32)
    query_grad = fold_keys(query_grad_piece, zero_heads)
    own_keys = key_rows.reshape(rows_here, head_count, HEAD_DIM)
    own_vals = val_rows.reshape(rows_here, head_count, HEAD_DIM)
    pieces = (queries, attn_grad, log_hi, log_lo, delta_hi, delta_lo)
    query_piece = lax.all_gather(pieces[0], ("ctx", "wa"), axis=0, tiled=True)
    grad_piece = lax.all_gather(pieces[1], ("ctx", "wa"), axis=0, tiled=True)
    log_high = lax.all_gather(pieces[2], ("ctx", "wa"), axis=0, tiled=True)
    log_low = lax.all_gather(pieces[3], ("ctx", "wa"), axis=0, tiled=True)
    delta_high = lax.all_gather(pieces[4], ("ctx", "wa"), axis=0, tiled=True)
    delta_low = lax.all_gather(pieces[5], ("ctx", "wa"), axis=0, tiled=True)
    piece_len = query_piece.shape[0]
    piece_place, piece_doc = token_places(
        jnp.arange(piece_len, dtype=jnp.int32), span_table, doc_ids
    )
    allowed = (query_doc[None, :] == piece_doc[:, None]) & (
        query_place[None, :] <= piece_place[:, None]
    )
    piece_heads = query_piece.reshape(piece_len, head_count, HEAD_DIM)
    piece_grads = grad_piece.reshape(piece_len, head_count, HEAD_DIM)
    piece_log = log_high.astype(jnp.float32) + log_low.astype(jnp.float32)
    piece_delta = delta_high.astype(jnp.float32) + delta_low.astype(jnp.float32)
    scores = (
        jnp.einsum("qhd,khd->hqk", piece_heads, own_keys, preferred_element_type=jnp.float32)
        * score_scale
    )
    exp_scores = jnp.exp(jnp.where(allowed[None], scores - piece_log.T[..., None], -jnp.inf))
    slopes = jnp.einsum("qhd,khd->hqk", piece_grads, own_vals, preferred_element_type=jnp.float32)
    score_grad = (exp_scores * (slopes - piece_delta.T[..., None])).astype(jnp.bfloat16)
    key_acc = jnp.einsum(
        "hqk,qhd->khd", score_grad, piece_heads, preferred_element_type=jnp.float32
    )
    val_acc = jnp.einsum(
        "hqk,qhd->khd",
        exp_scores.astype(jnp.bfloat16),
        piece_grads,
        preferred_element_type=jnp.float32,
    )
    here_cols = head_count * HEAD_DIM
    qkv_grad_own = jnp.concatenate(
        [
            (query_grad * score_scale).reshape(rows_here, here_cols),
            (key_acc * score_scale).reshape(rows_here, here_cols),
            val_acc.reshape(rows_here, here_cols),
        ],
        axis=1,
    ).astype(jnp.bfloat16)
    qkv_grad_full = row_gather(qkv_grad_own)
    grad_sums = jnp.sum(qkv_grad_full, axis=0, dtype=jnp.float32)
    query_bias_part = grad_sums[:model_width]
    value_bias_part = grad_sums[2 * model_width :]
    qkv_grad_loc = contract_rows(normed_cols, qkv_grad_full)
    normed_grad_cols = contract_cols(qkv_grad_full, qkv_weight)
    normed_grad = lax.all_gather(
        normed_grad_cols.astype(jnp.bfloat16), "wa", axis=1, tiled=True
    ).astype(normed_grad_cols.dtype)
    attn_gain_part = jnp.sum(normed_grad * attn_hat, axis=0)
    attn_shift_part = jnp.sum(normed_grad, axis=0)
    input_grad = (resid_grad + norm_back(normed_grad, attn_hat, attn_inv, attn_gain)).astype(
        jnp.bfloat16
    )
    qkv_grad_out, out_grad_turned, up_grad_turned, down_grad_out = (
        lax.psum_scatter(qkv_grad_loc, "ctx", scatter_dimension=1, tiled=True),
        lax.psum_scatter(out_grad_loc, "ctx", scatter_dimension=1, tiled=True),
        lax.psum_scatter(up_grad_loc, "ctx", scatter_dimension=1, tiled=True),
        lax.psum_scatter(down_grad_loc, "ctx", scatter_dimension=1, tiled=True),
    )
    packed = jnp.stack(
        [
            attn_gain_part,
            attn_shift_part,
            mlp_gain_part,
            mlp_shift_part,
            query_bias_part,
            value_bias_part,
            out_bias_part,
            down_bias_part,
        ]
    )
    packed_sum, up_bias_grad = lax.psum((packed, up_bias_part), "ctx")
    return (
        block_output,
        input_grad,
        qkv_grad_out,
        packed_sum[4],
        packed_sum[5],
        out_grad_turned.T,
        packed_sum[6],
        up_grad_turned.T,
        up_bias_grad,
        down_grad_out,
        packed_sum[7],
        packed_sum[0],
        packed_sum[1],
        packed_sum[2],
        packed_sum[3],
    )


def solution(mesh):
    placed = (
        P("ctx", None),
        P(),
        P(),
        P(),
        P(),
        P("wa", None),
        P(),
        P(),
        P(None, "wa"),
        P(),
        P(),
        P(),
        P(None, "wa"),
        P("wa"),
        P("wa", None),
        P(),
        P("ctx", None),
    )
    return jax.shard_map(
        body,
        mesh=mesh,
        in_specs=placed,
        out_specs=(
            P("ctx", "wa"),
            P("ctx", None),
            P("wa", "ctx"),
            P(),
            P(),
            P("ctx", "wa"),
            P(),
            P("ctx", "wa"),
            P("wa"),
            P("wa", "ctx"),
            P(),
            P(),
            P(),
            P(),
            P(),
        ),
        check_vma=False,
    )
```

profile of v0, /device:TPU:0, one launch (start us, length us, event | category | flops | bytes accessed | tf_op | source)
XLA Modules:
  0.0 826.9 jit_solution(8947178412588258652)
XLA Ops:
  7.2 1.3 convert_reduce_fusion.5
  8.5 0.8 dynamic-slice.9
  9.3 0.8 dynamic-slice.8
  10.7 1.0 subtract_multiply_fusion
  11.7 0.8 copy-done.15
  12.5 3.2 convolution_convert_fusion
  15.9 26.9 %reduce-scatter.14.cloned.1.call-done = bf16[32,3264]{1,0:T(8,128)(2,1)} async-done(((bf16[128,3264]{1,0:T(8,128)(2,1)}), bf16[32,3264]{1,0:T(8,128)(2,1)}) %reduce-scatter.14.cloned.1.call-update) | async-done | bytes 208912 | tf_op jit(solution)/shard_map/reduce_scatter | solution.py:100
  42.8 1.0 add_convert_fusion
  45.3 0.8 convert_element_type.134
  46.2 0.8 dynamic_slice.17
  47.0 8.8 %gather_fusion = s32[1024]{0:T(1024)S(1)} fusion(s32[8,2]{0,1:T(2,128)S(1)} %copy-done.1, s32[1024]{0:T(1024)S(1)} %bitcast.86), kind=kCustom, calls=%fused_computation | custom fusion | bytes 16384 | tf_op jit(solution)/shard_map/gather | solution.py:59
  55.9 0.8 gather_fusion.2
  56.7 4.5 gather_fusion.1
  62.2 40.2 %all-gather.9.cloned.1.call-done = bf16[1024,1088]{1,0:T(8,128)(2,1)} async-done(((bf16[32,1088]{1,0:T(8,128)(2,1)}), bf16[1024,1088]{1,0:T(8,128)(2,1)}) %all-gather.9.cloned.1.call-update) | async-done | bytes 2228240 | tf_op jit(solution)/shard_map/all_gather | solution.py:122
  102.5 4.2 copy.66
  106.7 2.4 select_reduce_fusion
  109.1 1.4 copy-done.4
  111.1 50.1 %all-gather.11.cloned.1.call-done = bf16[1024,1088]{1,0:T(8,128)(2,1)} async-done(((bf16[32,1088]{1,0:T(8,128)(2,1)}), bf16[1024,1088]{1,0:T(8,128)(2,1)}) %all-gather.11.cloned.1.call-update) | async-done | bytes 2228240 | tf_op jit(solution)/shard_map/all_gather | solution.py:123
  161.1 4.3 copy.68
  165.4 3.2 fusion.11
  168.8 14.0 %all_gather.40 = bf16[128,1088]{1,0:T(8,128)(2,1)S(1)} all-gather(bf16[32,1088]{1,0:T(8,128)(2,1)S(1)} %convert_element_type.141), channel_id=1, replica_groups=mesh['ctx'=8,'wa'=4] {'wa'}, dimensions={0}, use_global_device_ids=true | all-gather | bytes 348160 | tf_op jit(solution)/shard_map/all_gather | solution.py:108
  182.9 2.0 fusion.121
  184.9 14.1 %all_gather.41 = bf16[128,1088]{0,1:T(8,128)(2,1)S(1)} all-gather(bf16[128,272]{0,1:T(8,128)(2,1)S(1)} %get-tuple-element.55), channel_id=1, replica_groups=mesh['ctx'=8,'wa'=4] {'wa'}, dimensions={1}, use_global_device_ids=true | all-gather | bytes 348160 | tf_op jit(solution)/shard_map/all_gather | solution.py:181
  199.2 3.2 convolution_add_fusion
  202.4 1.6 fusion.122
  204.8 1.5 convolution_convert_fusion.1
  206.4 34.9 %all-reduce.8.cloned.1.call-done = bf16[128,1088]{0,1:T(8,128)(2,1)} async-done(((bf16[128,1088]{0,1:T(8,128)(2,1)}), bf16[128,1088]{0,1:T(8,128)(2,1)}) %all-reduce.8.cloned.1.call-update) | async-done | bytes 278544 | tf_op jit(solution)/shard_map/psum | solution.py:201
  241.3 2.1 fusion.59
  243.4 2.3 fusion.118
  245.6 0.8 copy-done.8
  246.5 1.1 convolution_convert_fusion.2
  248.2 19.8 %reduce-scatter.18.cloned.1.call-done = bf16[32,1088]{1,0:T(8,128)(2,1)} async-done(((bf16[128,1088]{1,0:T(8,128)(2,1)}), bf16[32,1088]{1,0:T(8,128)(2,1)}) %reduce-scatter.18.cloned.1.call-update) | async-done | bytes 69648 | tf_op jit(solution)/shard_map/reduce_scatter | solution.py:100
  268.0 1.4 compare_and_fusion
  269.4 0.8 reshape.638
  270.2 0.8 reshape.640
  271.1 1.8 reshape.643
  272.8 65.3 %all-gather.1 = bf16[32,32,17]{1,2,0:T(8,128)(2,1)S(1)} all-gather(bf16[1,32,17]{1,2,0:T(8,128)(2,1)S(1)} %bitcast.101), channel_id=1, replica_groups=mesh['ctx'=8,'wa'=4] {'ctx','wa'}, dimensions={0}, use_global_device_ids=true | all-gather | bytes 35904 | tf_op jit(solution)/shard_map/all_gather | solution.py:253
  338.1 67.5 %all-gather = bf16[32,32,17]{1,2,0:T(8,128)(2,1)S(1)} all-gather(bf16[1,32,17]{1,2,0:T(8,128)(2,1)S(1)} %bitcast.97), channel_id=1, replica_groups=mesh['ctx'=8,'wa'=4] {'ctx','wa'}, dimensions={0}, use_global_device_ids=true | all-gather | bytes 35904 | tf_op jit(solution)/shard_map/all_gather | solution.py:252
  405.9 1.8 convolution_convert_fusion.3
  407.8 4.3 copy.73
  412.1 3.5 fusion.65
  416.2 4.3 fusion.13
  420.7 65.1 %all-gather.3 = bf16[32,32,17]{1,2,0:T(8,128)(2,1)S(1)} all-gather(bf16[1,32,17]{1,2,0:T(8,128)(2,1)S(1)} %bitcast.102), channel_id=1, replica_groups=mesh['ctx'=8,'wa'=4] {'ctx','wa'}, dimensions={0}, use_global_device_ids=true | all-gather | bytes 35904 | tf_op jit(solution)/shard_map/all_gather | solution.py:255
  485.9 66.9 %all-gather.2 = bf16[32,32,17]{1,2,0:T(8,128)(2,1)S(1)} all-gather(bf16[1,32,17]{1,2,0:T(8,128)(2,1)S(1)} %copy.78), channel_id=1, replica_groups=mesh['ctx'=8,'wa'=4] {'ctx','wa'}, dimensions={0}, use_global_device_ids=true | all-gather | bytes 35904 | tf_op jit(solution)/shard_map/all_gather | solution.py:254
  553.1 4.3 copy.76
  557.4 3.0 fusion.15
  560.5 4.3 fusion.12
  565.2 0.8 concatenate.18
  566.0 17.8 %all_gather.48 = bf16[128,3264]{1,0:T(8,128)(2,1)S(1)} all-gather(bf16[32,3264]{1,0:T(8,128)(2,1)} %concatenate.18), channel_id=1, replica_groups=mesh['ctx'=8,'wa'=4] {'wa'}, dimensions={0}, use_global_device_ids=true | all-gather | bytes 1044480 | tf_op jit(solution)/shard_map/all_gather | solution.py:108
  583.8 3.4 fusion.113
  587.3 2.7 fusion.74
  590.1 4.4 fusion.71
  594.5 4.2 fusion.117
  598.8 1.4 dynamic_slice.18
  601.6 1.7 add_convert_fusion.1
  603.3 2.1 convolution_convert_fusion.5
  605.4 13.8 %all_gather.49 = bf16[128,1088]{0,1:T(8,128)(2,1)S(1)} all-gather(bf16[128,272]{0,1:T(8,128)(2,1)S(1)} %convolution_convert_fusion.5), channel_id=1, replica_groups=mesh['ctx'=8,'wa'=4] {'wa'}, dimensions={1}, use_global_device_ids=true | all-gather | bytes 348160 | tf_op jit(solution)/shard_map/all_gather | solution.py:298
  620.1 23.7 %all-reduce.4 = (f32[8,1088]{1,0:T(8,128)S(1)}, f32[1088]{0:T(1024)}) all-reduce(f32[8,1088]{1,0:T(8,128)S(1)} %stack.35, f32[1088]{0:T(1024)S(1)} %copy-done.47), channel_id=1, replica_groups=mesh['ctx'=8,'wa'=4] {'ctx'}, use_global_device_ids=true, to_apply=%region_23.24 | all-reduce | flops 9792 | bytes 78336 | tf_op jit(solution)/shard_map/psum | solution.py:324
  644.6 2.2 fusion.45
  646.8 13.7 %all-reduce.10.cloned.1.call-done = f32[272,3264]{1,0:T(8,128)} async-done(((f32[272,3264]{1,0:T(8,128)}), f32[272,3264]{1,0:T(8,128)}) %all-reduce.10.cloned.1.call-update) | async-done | bytes 3551248
  660.5 2.1 constant_dynamic-slice_fusion
  662.6 40.0 %reduce-scatter.20.cloned.1.call-done = f32[272,136]{0,1:T(8,128)} async-done(((f32[272,1088]{0,1:T(8,128)}), f32[272,136]{0,1:T(8,128)}) %reduce-scatter.20.cloned.1.call-update) | async-done | bytes 147984
  702.6 58.8 %reduce-scatter.22.cloned.1.call-done = f32[1088,136]{0,1:T(8,128)} async-done(((f32[1088,1088]{0,1:T(8,128)}), f32[1088,136]{0,1:T(8,128)}) %reduce-scatter.22.cloned.1.call-update) | async-done | bytes 591888
  761.4 58.7 %reduce-scatter.24.cloned.1.call-done = f32[1088,136]{0,1:T(8,128)} async-done(((f32[1088,1088]{0,1:T(8,128)}), f32[1088,136]{0,1:T(8,128)}) %reduce-scatter.24.cloned.1.call-update) | async-done | bytes 591888
  (187 shorter events, 10.1 us)
Async XLA Ops:
  7.2 195.2 %copy-start = (bf16[1088,1088]{1,0:T(8,128)(2,1)S(1)}, bf16[1088,1088]{1,0:T(8,128)(2,1)}, u32[]{:S(2)}) copy-start(bf16[1088,1088]{1,0:T(8,128)(2,1)} %param.31) | copy-start | bytes 7102468
  7.2 35.6 %reduce-scatter.14.cloned.1.call-start = ((), (), s32[]{:S(2)}) async-start(), calls=%async_computation.6 | async-start | bytes 1064960 | tf_op jit(solution)/shard_map/reduce_scatter | solution.py:100
  10.1 0.6 copy-start.41
  10.1 0.6 copy-start.43
  10.7 5.1 copy-start.45
  10.7 5.2 copy-start.46
  11.7 0.8 copy-start.15
  12.5 32.8 %copy-start.6 = (bf16[128,1088]{0,1:T(8,128)(2,1)S(1)}, bf16[128,1088]{0,1:T(8,128)(2,1)}, u32[]{:S(2)}) copy-start(bf16[128,1088]{0,1:T(8,128)(2,1)} %param.17) | copy-start | bytes 835588
  12.5 34.5 %copy-start.1 = (s32[8,2]{0,1:T(2,128)S(1)}, s32[8,2]{0,1:T(2,128)}, u32[]{:S(2)}) copy-start(s32[8,2]{0,1:T(2,128)} %param.18) | copy-start | bytes 196
  15.7 86.7 %all-gather.9.cloned.1.call-start = ((), (), s32[]{:S(2)}) async-start(), calls=%async_computation.7 | async-start | bytes 2433024 | tf_op jit(solution)/shard_map/all_gather | solution.py:122
  44.5 17.6 %copy-start.18 = (bf16[32,1088]{1,0:T(8,128)(2,1)}, bf16[32,1088]{1,0:T(8,128)(2,1)S(1)}, u32[]{:S(2)}) copy-start(bf16[32,1088]{1,0:T(8,128)(2,1)S(1)} %get-tuple-element.40) | copy-start | bytes 208900
  44.5 116.6 %all-gather.11.cloned.1.call-start = ((), (), s32[]{:S(2)}) async-start(), calls=%async_computation.8 | async-start | bytes 2433024 | tf_op jit(solution)/shard_map/all_gather | solution.py:123
  45.3 196.0 %all-reduce.8.cloned.1.call-start = ((), (), s32[]{:S(2)}) async-start(), calls=%async_computation.10 | async-start | bytes 557056 | tf_op jit(solution)/shard_map/psum | solution.py:201
  47.0 9.7 %copy-start.2 = (s32[1024]{0:T(1024)S(1)}, s32[1024]{0:T(1024)}, u32[]{:S(2)}) copy-start(s32[1024]{0:T(1024)} %param.19) | copy-start | bytes 12292
  56.7 5.3 copy-start.28
  61.2 45.5 %copy-start.29 = (s32[1024]{0:T(1024)}, s32[1024]{0:T(1024)S(1)}, u32[]{:S(2)}) copy-start(s32[1024]{0:T(1024)S(1)} %gather_fusion.1) | copy-start | bytes 12292
  61.9 44.8 %copy-start.48 = (s32[32]{0:T(128)}, s32[32]{0:T(128)S(1)}, u32[]{:S(2)}) copy-start(s32[32]{0:T(128)S(1)} %gather_fusion.3) | copy-start | bytes 388
  62.0 44.7 %copy-start.49 = (s32[32]{0:T(128)}, s32[32]{0:T(128)S(1)}, u32[]{:S(2)}) copy-start(s32[32]{0:T(128)S(1)} %fusion.95) | copy-start | bytes 388
  109.1 1.4 copy-start.4
  165.4 17.5 %copy-start.11 = (bf16[1088,272]{0,1:T(8,128)(2,1)S(1)}, bf16[1088,272]{0,1:T(8,128)(2,1)}, u32[]{:S(2)}) copy-start(bf16[1088,272]{0,1:T(8,128)(2,1)} %param.25) | copy-start | bytes 1775620
  168.6 30.6 %copy-start.26 = (f32[1088]{0:T(1024)S(1)}, f32[1088]{0:T(1024)}, u32[]{:S(2)}) copy-start(f32[1088]{0:T(1024)} %param.27) | copy-start | bytes 13060
  168.6 30.6 %copy-start.30 = (f32[1088]{0:T(1024)S(1)}, f32[1088]{0:T(1024)}, u32[]{:S(2)}) copy-start(f32[1088]{0:T(1024)} %param.28) | copy-start | bytes 13060
  168.8 30.4 %copy-start.21 = (bf16[32,1088]{1,0:T(8,128)(2,1)}, bf16[32,1088]{1,0:T(8,128)(2,1)S(1)}, u32[]{:S(2)}) copy-start(bf16[32,1088]{1,0:T(8,128)(2,1)S(1)} %convert_element_type.141) | copy-start | bytes 208900
  182.9 16.3 %copy-start.9 = (bf16[128,1088]{1,0:T(8,128)(2,1)}, bf16[128,1088]{1,0:T(8,128)(2,1)S(1)}, u32[]{:S(2)}) copy-start(bf16[128,1088]{1,0:T(8,128)(2,1)S(1)} %all_gather.40) | copy-start | bytes 835588
  184.9 17.5 %copy-start.16 = (bf16[128,1088]{0,1:T(8,128)(2,1)S(1)}, bf16[128,1088]{0,1:T(8,128)(2,1)}, u32[]{:S(2)}) copy-start(bf16[128,1088]{0,1:T(8,128)(2,1)} %param.33) | copy-start | bytes 835588
  199.0 44.4 %copy-start.3 = (bf16[128,1088]{0,1:T(8,128)(2,1)}, bf16[128,1088]{0,1:T(8,128)(2,1)S(1)}, u32[]{:S(2)}) copy-start(bf16[128,1088]{0,1:T(8,128)(2,1)S(1)} %all_gather.41) | copy-start | bytes 835588
  199.2 4.9 copy-start.37
  199.2 4.9 copy-start.39
  202.4 203.5 %copy-start.5 = (f32[128,1088]{0,1:T(8,128)}, f32[128,1088]{0,1:T(8,128)S(1)}, u32[]{:S(2)}) copy-start(f32[128,1088]{0,1:T(8,128)S(1)} %convolution_add_fusion) | copy-start | bytes 1671172
  202.4 2.3 copy-start.10
  204.0 0.7 copy-start.17
  206.3 63.1 %copy-start.20 = (bf16[32,1088]{1,0:T(8,128)(2,1)S(1)}, bf16[32,1088]{1,0:T(8,128)(2,1)}, u32[]{:S(2)}) copy-start(bf16[32,1088]{1,0:T(8,128)(2,1)} %get-tuple-element.42) | copy-start | bytes 208900
  206.3 64.0 %copy-start.19 = (bf16[32,1088]{1,0:T(8,128)(2,1)S(1)}, bf16[32,1088]{1,0:T(8,128)(2,1)}, u32[]{:S(2)}) copy-start(bf16[32,1088]{1,0:T(8,128)(2,1)} %get-tuple-element.41) | copy-start | bytes 208900
  206.3 61.6 %reduce-scatter.18.cloned.1.call-start = ((), (), s32[]{:S(2)}) async-start(), calls=%async_computation.11 | async-start | bytes 368640 | tf_op jit(solution)/shard_map/reduce_scatter | solution.py:100
  241.3 5.2 copy-start.12
  245.6 0.8 copy-start.8
  247.5 160.3 %all-gather.13.cloned.1.call-start = ((), (), s32[]{:S(2)}) async-start(), calls=%async_computation.12 | async-start | bytes 2433024 | tf_op jit(solution)/shard_map/all_gather | solution.py:250
  248.1 305.0 %all-gather.15.cloned.1.call-start = ((), (), s32[]{:S(2)}) async-start(), calls=%async_computation.13 | async-start | bytes 2433024 | tf_op jit(solution)/shard_map/all_gather | solution.py:251
  268.0 333.7 %reduce-scatter.16.cloned.1.call-start = ((), (), s32[]{:S(2)}) async-start(), calls=%async_computation.9 | async-start | bytes 348160 | tf_op jit(solution)/shard_map/reduce_scatter | solution.py:189
  407.7 4.4 copy-start.22
  407.7 252.8 %all-reduce.10.cloned.1.call-start = ((), (), s32[]{:S(2)}) async-start(), calls=%async_computation.14 | async-start | bytes 7241728
  412.1 3.5 copy-start.24
  412.1 3.6 copy-start.14
  553.1 4.3 copy-start.36
  557.4 3.1 copy-start.25
  587.2 2.8 copy-start.31
  587.2 2.8 copy-start.38
  587.2 2.8 copy-start.40
  587.2 115.4 %reduce-scatter.20.cloned.1.call-start = ((), (), s32[]{:S(2)}) async-start(), calls=%async_computation.15 | async-start | bytes 1880064
  590.0 171.4 %reduce-scatter.22.cloned.1.call-start = ((), (), s32[]{:S(2)}) async-start(), calls=%async_computation.16 | async-start | bytes 5640192
  594.4 225.7 %reduce-scatter.24.cloned.1.call-start = ((), (), s32[]{:S(2)}) async-start(), calls=%async_computation.17 | async-start | bytes 5640192
  598.7 1.5 copy-start.50
  598.7 2.8 copy-start.33
  598.7 2.8 copy-start.32
  598.7 2.8 copy-start.35
  598.7 2.8 copy-start.34
  598.8 2.9 copy-start.23
  598.8 20.5 %copy-start.27 = (f32[1088]{0:T(1024)S(1)}, f32[1088]{0:T(1024)}, u32[]{:S(2)}) copy-start(f32[1088]{0:T(1024)} %param.20) | copy-start | bytes 13060
  598.8 20.5 %copy-start.42 = (f32[128]{0:T(128)S(1)}, f32[128]{0:T(128)}, u32[]{:S(2)}) copy-start(f32[128]{0:T(128)} %copy-done.41) | copy-start | bytes 1540
  598.8 20.5 %copy-start.44 = (f32[128]{0:T(128)S(1)}, f32[128]{0:T(128)}, u32[]{:S(2)}) copy-start(f32[128]{0:T(128)} %copy-done.43) | copy-start | bytes 1540
  601.6 17.7 %copy-start.7 = (bf16[128,1088]{0,1:T(8,128)(2,1)S(1)}, bf16[128,1088]{0,1:T(8,128)(2,1)}, u32[]{:S(2)}) copy-start(bf16[128,1088]{0,1:T(8,128)(2,1)} %param.17) | copy-start | bytes 835588
  603.3 16.8 %copy-start.47 = (f32[1088]{0:T(1024)S(1)}, f32[1088]{0:T(1024)}, u32[]{:S(2)}) copy-start(f32[1088]{0:T(1024)} %get-tuple-element.57) | copy-start | bytes 13060
  619.3 0.7 copy-start.13
Sparse Core Ops, SparseCore 0:
  15.9 26.9 reduce-scatter.13
  46.2 56.2 all-gather.8
  105.3 55.8 all-gather.10
  206.4 34.7 all-reduce.7
  247.7 20.2 reduce-scatter.17
  270.6 55.5 all-gather.12
  329.0 55.9 all-gather.14
  407.8 17.8 reduce-scatter.15
  587.3 73.1 all-reduce.9
  664.2 38.3 reduce-scatter.19
  706.7 54.7 reduce-scatter.21
  765.3 54.7 reduce-scatter.23
where the time goes:
time: 828 us; the launch traced here: 827 us
  blocking collectives  348 us (42%)
  waiting for transfers between devices  344 us (42%)
  matrix products  51.8 us (6%)
  local copies, waits for them, and re-layouts  50.5 us (6%)
  other arithmetic  15.7 us (2%)
  between operations  15.7 us (2%)
    unnamed x16, waiting for transfers between devices  173 us
    all_gather x1, blocking collectives, body(): log_high = lax.all_gather(pieces[2], ('ctx', 'wa'), axis=0, tiled=True)  67.5 us
    all_gather x1, blocking collectives, body(): delta_high = lax.all_gather(pieces[4], ('ctx', 'wa'), axis=0, tiled=True)  66.9 us
    all_gather x1, blocking collectives, body(): log_low = lax.all_gather(pieces[3], ('ctx', 'wa'), axis=0, tiled=True)  65.3 us
    all_gather x1, blocking collectives, body(): delta_low = lax.all_gather(pieces[5], ('ctx', 'wa'), axis=0, tiled=True)  65.1 us
    all_gather x1, waiting for transfers between devices, fold_keys(): lax.all_gather(val_rows, ('ctx', 'wa'), axis=0, tiled=True)  50.1 us
    reduce_scatter x2, waiting for transfers between devices, row_sums(): lax.psum_scatter(term_fn(jnp.int32(0), lax.axis_size('wa') * rows_here).a...  46.7 us
    all_gather x1, waiting for transfers between devices, fold_keys(): lax.all_gather(key_rows, ('ctx', 'wa'), axis=0, tiled=True)  40.2 us
  transfers between devices with their start and end apart: 12, of which 9 were waited for; matrix products, arithmetic and copies ran while one was open for 10% of the time, Pallas kernels for 0%

commit v1 on v0

--- a/solution.py
+++ b/solution.py
@@ -10,6 +10,18 @@
 norm_eps = 1e-05
 root_half = 0.7071067811865476
 inv_root_tau = 0.3989422804014327
+
+
+def gather_by_bits(array, axis, dim):
+    ways, here = (lax.axis_size(axis), lax.axis_index(axis))
+    grown, reach = (array, 1)
+    while reach < ways:
+        theirs = lax.ppermute(grown, axis, [(d, d ^ reach) for d in range(ways)])
+        mine_first = jnp.concatenate([grown, theirs], axis=dim)
+        theirs_first = jnp.concatenate([theirs, grown], axis=dim)
+        grown = jnp.where(here & reach == 0, mine_first, theirs_first)
+        reach = 2 * reach
+    return grown
 
 
 def rounded(value):
@@ -119,7 +131,7 @@
         return fold_fn(
             init,
             (
-                lax.all_gather(key_rows, ("ctx", "wa"), axis=0, tiled=True),
+                gather_by_bits(key_rows, ("ctx", "wa"), 0),
                 lax.all_gather(val_rows, ("ctx", "wa"), axis=0, tiled=True),
             ),
             jnp.int32(0),

time: 828 us -> 790 us (0.954)
  waiting for transfers between devices: 344 us -> 292 us
  other arithmetic: 15.7 us -> 25.9 us
    all_gather x1, waiting for transfers between devices: 50.1 us -> 0.02 us  [fold_keys(): lax.all_gather(val_rows, ('ctx', 'wa'), axis=0, tiled=True)]
    all_gather x1 -> x0, waiting for transfers between devices: 40.2 us -> none  [fold_keys(): lax.all_gather(key_rows, ('ctx', 'wa'), axis=0, tiled=True)]
    ppermute x0 -> x5, waiting for transfers between devices: none -> 35.8 us  [gather_by_bits(): theirs = lax.ppermute(grown, axis, [(d, d ^ reach) for d in range(ways)])]
    unnamed x16 -> x15, waiting for transfers between devices: 173 us -> 173 us
  transfers between devices with their start and end apart: 12 -> 16, of which waited for: 9 -> 11; matrix products, arithmetic and copies ran while one was open for 10% -> 12% of each run, Pallas kernels for 0% -> 0%
where the time goes in v1:
time: 790 us; the launch traced here: 788 us
  blocking collectives  349 us (44%)
  waiting for transfers between devices  292 us (37%)
  local copies, waits for them, and re-layouts  54.7 us (7%)
  matrix products  47 us (6%)
  other arithmetic  25.9 us (3%)
  between operations  15.6 us (2%)
    unnamed x15, waiting for transfers between devices  173 us
    all_gather x1, blocking collectives, body(): log_high = lax.all_gather(pieces[2], ('ctx', 'wa'), axis=0, tiled=True)  67.7 us
    all_gather x1, blocking collectives, body(): delta_high = lax.all_gather(pieces[4], ('ctx', 'wa'), axis=0, tiled=True)  67.3 us
    all_gather x1, blocking collectives, body(): log_low = lax.all_gather(pieces[3], ('ctx', 'wa'), axis=0, tiled=True)  65.3 us
    all_gather x1, blocking collectives, body(): delta_low = lax.all_gather(pieces[5], ('ctx', 'wa'), axis=0, tiled=True)  64.9 us
    reduce_scatter x2, waiting for transfers between devices, row_sums(): lax.psum_scatter(term_fn(jnp.int32(0), lax.axis_size('wa') * rows_here).a...  46.6 us
    psum x1, waiting for transfers between devices, body(): lax.psum(contract_cols(hidden_grad_b, up_weight).astype(jnp.bfloat16), 'wa')  36.3 us
    ppermute x5, waiting for transfers between devices, gather_by_bits(): theirs = lax.ppermute(grown, axis, [(d, d ^ reach) for d in range(ways)])  35.8 us
  transfers between devices with their start and end apart: 16, of which 11 were waited for; matrix products, arithmetic and copies ran while one was open for 12% of the time, Pallas kernels for 0%

profile of v1, /device:TPU:0, one launch (start us, length us, event | category | flops | bytes accessed | tf_op | source)
XLA Modules:
  0.0 788.4 jit_solution(4084652596925273678)
XLA Ops:
  7.2 1.3 convert_reduce_fusion.5
  10.1 1.0 subtract_multiply_fusion
  12.0 3.2 convolution_convert_fusion
  15.4 26.9 %reduce-scatter.14.cloned.1.call-done = bf16[32,3264]{1,0:T(8,128)(2,1)} async-done(((bf16[128,3264]{1,0:T(8,128)(2,1)}), bf16[32,3264]{1,0:T(8,128)(2,1)}) %reduce-scatter.14.cloned.1.call-update) | async-done | bytes 208912 | tf_op jit(solution)/shard_map/reduce_scatter | solution.py:112
  44.0 4.3 collective-permute-done
  49.2 6.8 collective-permute-done.1
  57.7 1.3 dynamic_slice.17
  59.1 8.8 %gather_fusion = s32[1024]{0:T(1024)S(1)} fusion(s32[8,2]{0,1:T(2,128)S(1)} %copy-done.2, s32[1024]{0:T(1024)S(1)} %bitcast.88), kind=kCustom, calls=%fused_computation | custom fusion | bytes 16384 | tf_op jit(solution)/shard_map/gather | solution.py:71
  68.5 1.3 maximum_select_fusion.3
  69.8 1.0 copy.85
  70.8 1.4 collective-permute-start.3
  72.3 1.3 gather_fusion.2
  74.9 5.0 gather_fusion.1
  79.9 6.3 collective-permute-done.3
  86.1 2.2 copy.86
  88.3 2.7 maximum_select_fusion.1
  91.0 2.4 copy.88
  93.4 1.6 collective-permute-start.4
  97.8 1.4 maximum_select_fusion.8
  99.6 1.6 maximum_select_fusion.2
  101.2 18.5 %collective-permute-done.4 = bf16[512,1088]{0,1:T(8,128)(2,1)} collective-permute-done((bf16[512,1088]{0,1:T(8,128)(2,1)}, bf16[512,1088]{0,1:T(8,128)(2,1)}, u32[]{:S(2)}, u32[]{:S(2)}) %collective-permute-start.4) | collective-permute-done | bytes 1114144 | tf_op jit(solution)/shard_map/ppermute | solution.py:19
  119.7 2.7 select_reduce_fusion
  122.4 1.4 copy-done.17
  124.5 4.2 copy.90
  128.8 3.2 fusion.11
  132.2 14.0 %all_gather.35 = bf16[128,1088]{1,0:T(8,128)(2,1)S(1)} all-gather(bf16[32,1088]{1,0:T(8,128)(2,1)S(1)} %convert_element_type.141), channel_id=1, replica_groups=mesh['ctx'=8,'wa'=4] {'wa'}, dimensions={0}, use_global_device_ids=true | all-gather | bytes 348160 | tf_op jit(solution)/shard_map/all_gather | solution.py:120
  146.2 2.0 fusion.123
  148.3 14.2 %all_gather.36 = bf16[128,1088]{0,1:T(8,128)(2,1)S(1)} all-gather(bf16[128,272]{0,1:T(8,128)(2,1)S(1)} %get-tuple-element.55), channel_id=1, replica_groups=mesh['ctx'=8,'wa'=4] {'wa'}, dimensions={1}, use_global_device_ids=true | all-gather | bytes 348160 | tf_op jit(solution)/shard_map/all_gather | solution.py:193
  162.8 3.2 convolution_add_fusion
  166.0 1.6 fusion.124
  168.3 1.5 convolution_convert_fusion.1
  169.9 36.3 %all-reduce.8.cloned.1.call-done = bf16[128,1088]{0,1:T(8,128)(2,1)} async-done(((bf16[128,1088]{0,1:T(8,128)(2,1)}), bf16[128,1088]{0,1:T(8,128)(2,1)}) %all-reduce.8.cloned.1.call-update) | async-done | bytes 278544 | tf_op jit(solution)/shard_map/psum | solution.py:213
  206.2 2.1 fusion.59
  208.3 2.3 fusion.120
  211.4 1.1 convolution_convert_fusion.2
  213.1 19.8 %reduce-scatter.18.cloned.1.call-done = bf16[32,1088]{1,0:T(8,128)(2,1)} async-done(((bf16[128,1088]{1,0:T(8,128)(2,1)}), bf16[32,1088]{1,0:T(8,128)(2,1)}) %reduce-scatter.18.cloned.1.call-update) | async-done | bytes 69648 | tf_op jit(solution)/shard_map/reduce_scatter | solution.py:112
  232.9 1.4 compare_and_fusion
  236.0 65.3 %all-gather.1 = bf16[32,32,17]{1,2,0:T(8,128)(2,1)S(1)} all-gather(bf16[1,32,17]{1,2,0:T(8,128)(2,1)S(1)} %bitcast.104), channel_id=1, replica_groups=mesh['ctx'=8,'wa'=4] {'ctx','wa'}, dimensions={0}, use_global_device_ids=true | all-gather | bytes 35904 | tf_op jit(solution)/shard_map/all_gather | solution.py:265
  301.3 67.7 %all-gather = bf16[32,32,17]{1,2,0:T(8,128)(2,1)S(1)} all-gather(bf16[1,32,17]{1,2,0:T(8,128)(2,1)S(1)} %bitcast.100), channel_id=1, replica_groups=mesh['ctx'=8,'wa'=4] {'ctx','wa'}, dimensions={0}, use_global_device_ids=true | all-gather | bytes 35904 | tf_op jit(solution)/shard_map/all_gather | solution.py:264
  369.9 1.0 reshape.656
  370.9 1.8 convolution_convert_fusion.3
  372.8 3.0 copy.95
  375.8 1.8 fusion.66
  378.2 5.3 fusion.13
  383.8 64.9 %all-gather.3 = bf16[32,32,17]{1,2,0:T(8,128)(2,1)S(1)} all-gather(bf16[1,32,17]{1,2,0:T(8,128)(2,1)S(1)} %bitcast.105), channel_id=1, replica_groups=mesh['ctx'=8,'wa'=4] {'ctx','wa'}, dimensions={0}, use_global_device_ids=true | all-gather | bytes 35904 | tf_op jit(solution)/shard_map/all_gather | solution.py:267
  448.8 67.3 %all-gather.2 = bf16[32,32,17]{1,2,0:T(8,128)(2,1)S(1)} all-gather(bf16[1,32,17]{1,2,0:T(8,128)(2,1)S(1)} %copy.100), channel_id=1, replica_groups=mesh['ctx'=8,'wa'=4] {'ctx','wa'}, dimensions={0}, use_global_device_ids=true | all-gather | bytes 35904 | tf_op jit(solution)/shard_map/all_gather | solution.py:266
  516.3 4.2 copy.98
  520.6 3.1 fusion.15
  523.7 3.7 fusion.12
  527.9 17.6 %all_gather.43 = bf16[128,3264]{1,0:T(8,128)(2,1)S(1)} all-gather(bf16[32,3264]{1,0:T(8,128)(2,1)S(1)} %concatenate.109), channel_id=1, replica_groups=mesh['ctx'=8,'wa'=4] {'wa'}, dimensions={0}, use_global_device_ids=true | all-gather | bytes 1044480 | tf_op jit(solution)/shard_map/all_gather | solution.py:120
  545.5 3.5 fusion.115
  550.0 2.5 fusion.74
  552.6 3.2 fusion.71
  556.9 3.1 fusion.119
  562.4 1.6 add_convert_fusion.1
  564.7 14.0 %all_gather.44 = bf16[128,1088]{0,1:T(8,128)(2,1)S(1)} all-gather(bf16[128,272]{0,1:T(8,128)(2,1)S(1)} %convolution_convert_fusion.5), channel_id=1, replica_groups=mesh['ctx'=8,'wa'=4] {'wa'}, dimensions={1}, use_global_device_ids=true | all-gather | bytes 348160 | tf_op jit(solution)/shard_map/all_gather | solution.py:310
  578.7 1.5 fusion.60
  580.5 23.9 %all-reduce.4 = (f32[8,1088]{1,0:T(8,128)S(1)}, f32[1088]{0:T(1024)}) all-reduce(f32[8,1088]{1,0:T(8,128)S(1)} %stack.35, f32[1088]{0:T(1024)S(1)} %copy-done.64), channel_id=1, replica_groups=mesh['ctx'=8,'wa'=4] {'ctx'}, use_global_device_ids=true, to_apply=%region_23.24 | all-reduce | flops 9792 | bytes 78336 | tf_op jit(solution)/shard_map/psum | solution.py:336
  605.1 2.3 fusion.45
  607.5 14.6 %all-reduce.10.cloned.1.call-done = f32[272,3264]{1,0:T(8,128)} async-done(((f32[272,3264]{1,0:T(8,128)}), f32[272,3264]{1,0:T(8,128)}) %all-reduce.10.cloned.1.call-update) | async-done | bytes 3551248
  622.1 2.1 constant_dynamic-slice_fusion
  624.2 40.2 %reduce-scatter.20.cloned.1.call-done = f32[272,136]{0,1:T(8,128)} async-done(((f32[272,1088]{0,1:T(8,128)}), f32[272,136]{0,1:T(8,128)}) %reduce-scatter.20.cloned.1.call-update) | async-done | bytes 147984
  664.4 58.7 %reduce-scatter.22.cloned.1.call-done = f32[1088,136]{0,1:T(8,128)} async-done(((f32[1088,1088]{0,1:T(8,128)}), f32[1088,136]{0,1:T(8,128)}) %reduce-scatter.22.cloned.1.call-update) | async-done | bytes 591888
  723.0 58.8 %reduce-scatter.24.cloned.1.call-done = f32[1088,136]{0,1:T(8,128)} async-done(((f32[1088,1088]{0,1:T(8,128)}), f32[1088,136]{0,1:T(8,128)}) %reduce-scatter.24.cloned.1.call-update) | async-done | bytes 591888
  (242 shorter events, 24.9 us)
Async XLA Ops:
  7.2 158.8 %copy-start = (bf16[1088,1088]{1,0:T(8,128)(2,1)S(1)}, bf16[1088,1088]{1,0:T(8,128)(2,1)}, u32[]{:S(2)}) copy-start(bf16[1088,1088]{1,0:T(8,128)(2,1)} %param.31) | copy-start | bytes 7102468
  7.2 35.1 %reduce-scatter.14.cloned.1.call-start = ((), (), s32[]{:S(2)}) async-start(), calls=%async_computation.6 | async-start | bytes 1064960 | tf_op jit(solution)/shard_map/reduce_scatter | solution.py:112
  10.1 5.1 copy-start.40
  10.1 5.1 copy-start.57
  10.1 5.1 copy-start.59
  10.1 5.2 copy-start.62
  10.1 5.2 copy-start.63
  12.0 44.9 %copy-start.9 = (bf16[128,1088]{0,1:T(8,128)(2,1)S(1)}, bf16[128,1088]{0,1:T(8,128)(2,1)}, u32[]{:S(2)}) copy-start(bf16[128,1088]{0,1:T(8,128)(2,1)} %param.17) | copy-start | bytes 835588
  15.2 43.9 %copy-start.2 = (s32[8,2]{0,1:T(2,128)S(1)}, s32[8,2]{0,1:T(2,128)}, u32[]{:S(2)}) copy-start(s32[8,2]{0,1:T(2,128)} %param.18) | copy-start | bytes 196
  15.2 109.3 %all-gather.8.cloned.1.call-start = ((), (), s32[]{:S(2)}) async-start(), calls=%async_computation.7 | async-start | bytes 2433024 | tf_op jit(solution)/shard_map/all_gather | solution.py:135
  43.9 5.3 copy-start.27
  43.9 4.4 collective-permute-start
  44.0 162.2 %all-reduce.8.cloned.1.call-start = ((), (), s32[]{:S(2)}) async-start(), calls=%async_computation.9 | async-start | bytes 557056 | tf_op jit(solution)/shard_map/psum | solution.py:213
  48.3 7.7 collective-permute-start.1
  56.7 11.2 %copy-start.19 = (bf16[128,1088]{1,0:T(8,128)(2,1)}, bf16[128,1088]{1,0:T(8,128)(2,1)S(1)}, u32[]{:S(2)}) copy-start(bf16[128,1088]{1,0:T(8,128)(2,1)S(1)} %maximum_select_fusion.7) | copy-start | bytes 835588
  56.7 11.8 %collective-permute-start.2 = (bf16[128,1088]{1,0:T(8,128)(2,1)S(1)}, bf16[128,1088]{1,0:T(8,128)(2,1)S(1)}, u32[]{:S(2)}, u32[]{:S(2)}) collective-permute-start(bf16[128,1088]{1,0:T(8,128)(2,1)S(1)} %maximum_select_fusion.7), channel_id=1, source_target_pairs={{0,4},{1,5},{2,6},{3,7},{4,0},{5,1},{6,2},{7,3},{8,12},{9,13},{10,... | collective-permute-start | bytes 835592 | tf_op jit(solution)/shard_map/ppermute | solution.py:19
  67.9 6.9 copy-start.3
  70.8 15.3 %collective-permute-start.3 = (bf16[256,1088]{0,1:T(8,128)(2,1)}, bf16[256,1088]{0,1:T(8,128)(2,1)}, u32[]{:S(2)}, u32[]{:S(2)}) collective-permute-start(bf16[256,1088]{0,1:T(8,128)(2,1)} %copy.85), channel_id=1, source_target_pairs={{0,8},{1,9},{2,10},{3,11},{4,12},{5,13},{6,14},{7,15},{8,0},{9,1},... | collective-permute-start | bytes 1671176 | tf_op jit(solution)/shard_map/ppermute | solution.py:19
  79.9 15.9 %copy-start.44 = (s32[1024]{0:T(1024)}, s32[1024]{0:T(1024)S(1)}, u32[]{:S(2)}) copy-start(s32[1024]{0:T(1024)S(1)} %gather_fusion.1) | copy-start | bytes 12292
  88.3 7.4 copy-start.43
  91.0 4.0 copy-start.67
  91.0 4.9 copy-start.25
  91.0 5.9 copy-start.31
  93.4 26.3 %collective-permute-start.4 = (bf16[512,1088]{0,1:T(8,128)(2,1)}, bf16[512,1088]{0,1:T(8,128)(2,1)}, u32[]{:S(2)}, u32[]{:S(2)}) collective-permute-start(bf16[512,1088]{0,1:T(8,128)(2,1)} %copy.88), channel_id=1, source_target_pairs={{0,16},{1,17},{2,18},{3,19},{4,20},{5,21},{6,22},{7,23},{8,24},{9,... | collective-permute-start | bytes 3342344 | tf_op jit(solution)/shard_map/ppermute | solution.py:19
  95.7 5.5 copy-start.65
  95.9 26.5 %copy-start.37 = (pred[32,1024]{1,0:T(8,128)(4,1)}, pred[32,1024]{1,0:T(8,128)(4,1)S(1)}, u32[]{:S(2)}) copy-start(pred[32,1024]{1,0:T(8,128)(4,1)S(1)} %compare_and_fusion.1) | copy-start | bytes 98308
  101.2 21.2 %copy-start.22 = (bf16[512,17,64]{0,2,1:T(8,128)(2,1)}, bf16[512,17,64]{0,2,1:T(8,128)(2,1)S(1)}, u32[]{:S(2)}) copy-start(bf16[512,17,64]{0,2,1:T(8,128)(2,1)S(1)} %maximum_select_fusion.2) | copy-start | bytes 3342340
  124.5 4.3 copy-start.38
  128.7 17.5 %copy-start.14 = (bf16[1088,272]{0,1:T(8,128)(2,1)S(1)}, bf16[1088,272]{0,1:T(8,128)(2,1)}, u32[]{:S(2)}) copy-start(bf16[1088,272]{0,1:T(8,128)(2,1)} %param.25) | copy-start | bytes 1775620
  128.7 17.5 %copy-start.61 = (f32[272]{0:T(512)S(1)}, f32[272]{0:T(512)}, u32[]{:S(2)}) copy-start(f32[272]{0:T(512)} %dynamic_slice.17) | copy-start | bytes 3268
  131.9 30.8 %copy-start.36 = (f32[1088]{0:T(1024)S(1)}, f32[1088]{0:T(1024)}, u32[]{:S(2)}) copy-start(f32[1088]{0:T(1024)} %param.27) | copy-start | bytes 13060
  131.9 30.8 %copy-start.45 = (f32[1088]{0:T(1024)S(1)}, f32[1088]{0:T(1024)}, u32[]{:S(2)}) copy-start(f32[1088]{0:T(1024)} %param.28) | copy-start | bytes 13060
  132.0 30.8 %copy-start.56 = (f32[1088]{0:T(1024)S(1)}, f32[1088]{0:T(1024)}, u32[]{:S(2)}) copy-start(f32[1088]{0:T(1024)} %param.30) | copy-start | bytes 13060
  132.2 16.1 %copy-start.29 = (bf16[32,1088]{1,0:T(8,128)(2,1)}, bf16[32,1088]{1,0:T(8,128)(2,1)S(1)}, u32[]{:S(2)}) copy-start(bf16[32,1088]{1,0:T(8,128)(2,1)S(1)} %convert_element_type.141) | copy-start | bytes 208900
  146.2 16.5 %copy-start.11 = (bf16[128,1088]{1,0:T(8,128)(2,1)}, bf16[128,1088]{1,0:T(8,128)(2,1)S(1)}, u32[]{:S(2)}) copy-start(bf16[128,1088]{1,0:T(8,128)(2,1)S(1)} %all_gather.35) | copy-start | bytes 835588
  148.3 17.7 %copy-start.20 = (bf16[128,1088]{0,1:T(8,128)(2,1)S(1)}, bf16[128,1088]{0,1:T(8,128)(2,1)}, u32[]{:S(2)}) copy-start(bf16[128,1088]{0,1:T(8,128)(2,1)} %param.33) | copy-start | bytes 835588
  162.5 45.8 %copy-start.4 = (bf16[128,1088]{0,1:T(8,128)(2,1)}, bf16[128,1088]{0,1:T(8,128)(2,1)S(1)}, u32[]{:S(2)}) copy-start(bf16[128,1088]{0,1:T(8,128)(2,1)S(1)} %all_gather.36) | copy-start | bytes 835588
  162.7 4.9 copy-start.52
  162.7 4.9 copy-start.54
  166.0 205.0 %copy-start.6 = (f32[128,1088]{0,1:T(8,128)}, f32[128,1088]{0,1:T(8,128)S(1)}, u32[]{:S(2)}) copy-start(f32[128,1088]{0,1:T(8,128)S(1)} %convolution_add_fusion) | copy-start | bytes 1671172
  169.8 64.5 %copy-start.28 = (bf16[32,1088]{1,0:T(8,128)(2,1)S(1)}, bf16[32,1088]{1,0:T(8,128)(2,1)}, u32[]{:S(2)}) copy-start(bf16[32,1088]{1,0:T(8,128)(2,1)} %copy-done.27) | copy-start | bytes 208900
  169.8 65.3 %copy-start.26 = (bf16[32,1088]{1,0:T(8,128)(2,1)S(1)}, bf16[32,1088]{1,0:T(8,128)(2,1)}, u32[]{:S(2)}) copy-start(bf16[32,1088]{1,0:T(8,128)(2,1)} %get-tuple-element.41) | copy-start | bytes 208900
  169.8 63.0 %reduce-scatter.18.cloned.1.call-start = ((), (), s32[]{:S(2)}) async-start(), calls=%async_computation.10 | async-start | bytes 368640 | tf_op jit(solution)/shard_map/reduce_scatter | solution.py:112
  206.2 5.2 copy-start.15
  212.5 160.3 %all-gather.10.cloned.1.call-start = ((), (), s32[]{:S(2)}) async-start(), calls=%async_computation.11 | async-start | bytes 2433024 | tf_op jit(solution)/shard_map/all_gather | solution.py:262
  213.1 303.3 %all-gather.12.cloned.1.call-start = ((), (), s32[]{:S(2)}) async-start(), calls=%async_computation.12 | async-start | bytes 2433024 | tf_op jit(solution)/shard_map/all_gather | solution.py:263
  232.9 329.5 %reduce-scatter.16.cloned.1.call-start = ((), (), s32[]{:S(2)}) async-start(), calls=%async_computation.8 | async-start | bytes 348160 | tf_op jit(solution)/shard_map/reduce_scatter | solution.py:201
  372.7 249.4 %all-reduce.10.cloned.1.call-start = ((), (), s32[]{:S(2)}) async-start(), calls=%async_computation.13 | async-start | bytes 7241728
  516.3 4.3 copy-start.39
  516.3 4.3 copy-start.51
  527.4 18.1 %copy-start.41 = (f32[272]{0:T(512)S(1)}, f32[272]{0:T(512)}, u32[]{:S(2)}) copy-start(f32[272]{0:T(512)} %copy-done.40) | copy-start | bytes 3268
  549.0 3.5 copy-start.5
  549.1 3.5 copy-start.24
  549.1 3.5 copy-start.46
  549.1 3.5 copy-start.53
  549.1 115.3 %reduce-scatter.20.cloned.1.call-start = ((), (), s32[]{:S(2)}) async-start(), calls=%async_computation.14 | async-start | bytes 1880064
  552.5 170.5 %reduce-scatter.22.cloned.1.call-start = ((), (), s32[]{:S(2)}) async-start(), calls=%async_computation.15 | async-start | bytes 5640192
  555.8 226.0 %reduce-scatter.24.cloned.1.call-start = ((), (), s32[]{:S(2)}) async-start(), calls=%async_computation.16 | async-start | bytes 5640192
  560.1 4.0 copy-start.8
  560.1 18.6 %copy-start.42 = (f32[1088]{0:T(1024)S(1)}, f32[1088]{0:T(1024)}, u32[]{:S(2)}) copy-start(f32[1088]{0:T(1024)} %param.20) | copy-start | bytes 13060
  560.1 18.6 %copy-start.58 = (f32[128]{0:T(128)S(1)}, f32[128]{0:T(128)}, u32[]{:S(2)}) copy-start(f32[128]{0:T(128)} %copy-done.57) | copy-start | bytes 1540
  560.1 18.6 %copy-start.60 = (f32[128]{0:T(128)S(1)}, f32[128]{0:T(128)}, u32[]{:S(2)}) copy-start(f32[128]{0:T(128)} %copy-done.59) | copy-start | bytes 1540
  564.1 16.5 %copy-start.64 = (f32[1088]{0:T(1024)S(1)}, f32[1088]{0:T(1024)}, u32[]{:S(2)}) copy-start(f32[1088]{0:T(1024)} %get-tuple-element.57) | copy-start | bytes 13060
  564.7 217.2 %copy-start.1 = (bf16[1088,1088]{1,0:T(8,128)(2,1)S(1)}, bf16[1088,1088]{1,0:T(8,128)(2,1)}, u32[]{:S(2)}) copy-start(bf16[1088,1088]{1,0:T(8,128)(2,1)} %param.31) | copy-start | bytes 7102468
  (21 other events, 37.8 us)
Sparse Core Ops, SparseCore 0:
  15.3 26.9 reduce-scatter.13
  45.1 57.0 all-gather.7
  170.0 36.1 all-reduce.7
  212.6 20.2 reduce-scatter.17
  235.5 55.3 all-gather.9
  293.6 56.1 all-gather.11
  372.8 17.5 reduce-scatter.15
  549.2 72.8 all-reduce.9
  626.0 38.3 reduce-scatter.19
  668.3 54.7 reduce-scatter.21
  727.1 54.7 reduce-scatter.23
